TPU v7x, 32 devices: a whole 2x2x4 slice. The times are simulated.
32 devices in a mesh: row: 4 (over x, core), col: 8 (over z, y).
Axes of the slice: x: 2, y: 2, z: 4, core: 2. Of those that a mesh axis runs over, the one named last changes fastest.
Arguments:
- rhs: float32 [32768, 512], P('col', 'row'), may hold values from -6 to 6
- factors: bfloat16 [32768, 2048], P('col', 'row'), may hold values from -0.15625 to 0.15625
- diag_inv: float32 [4, 512, 512], replicated, may hold values from -2 to 2, as said below
Outputs:
- solution: float32 [32768, 512], P('col', 'row')
Inputs may be any that keep to these rules, and one draw needn't show every extreme that they name: `diag_inv`: entries off the diagonal of each block lie within 2 / sqrt(512) in magnitude; diagonal entries lie in 0.5 to 2.
All inputs are finite; a program needn't handle non-finite values.
Results may differ from a plain program's by a relative error of at most 0.0038.
Values may be sent and summed in bfloat16 or wider, within the bound.
A program may use at most 128 MiB of HBM per device.

v0:
```python
import jax
import jax.numpy as jnp
from jax import lax
from jax.sharding import PartitionSpec as P


def body(rhs, factors, diag_inv):
    rows_dev = rhs.shape[0]
    steps = diag_inv.shape[0]
    block = diag_inv.shape[1]
    col_count = lax.axis_size("col")
    block_span = rows_dev * col_count // steps
    my_index = lax.axis_index("col")
    global_rows = my_index * rows_dev + jnp.arange(rows_dev)
    index = jnp.arange(block)
    strict_lower = index[:, None] > index[None, :]
    eye = jnp.eye(block, dtype=jnp.float32)
    panel_rows = lax.all_gather(factors, "row", axis=1, tiled=True)

    def solve_block(matrix, work, step):
        owner_index = step * col_count // steps
        owner = my_index == owner_index
        product = jnp.dot(
            matrix,
            work[:block],
            precision=lax.Precision.HIGHEST,
            preferred_element_type=jnp.float32,
        )
        solved = lax.psum(jnp.where(owner, product, jnp.float32(0.0)), "col")
        return (solved, owner)

    def apply_update(work, solved, owner, columns, row_mask):
        product = jnp.dot(columns, solved.astype(jnp.bfloat16), preferred_element_type=jnp.float32)
        updated = jnp.where(row_mask[:, None], work - product, work)
        leading = jnp.where(owner, solved, updated[:block])
        return jnp.concatenate([leading, updated[block:]], axis=0)

    work = rhs
    kept_columns = []
    for step in range(steps):
        lower_inv = jnp.where(strict_lower, diag_inv[step], jnp.float32(0.0)) + eye
        solved, owner = solve_block(lower_inv, work, step)
        columns = panel_rows[:, step * block : (step + 1) * block]
        kept_columns.append(columns)
        row_mask = global_rows >= step * block_span + block
        work = apply_update(work, solved, owner, columns, row_mask)
    for step in reversed(range(steps)):
        upper_inv = jnp.triu(diag_inv[step])
        solved, owner = solve_block(upper_inv, work, step)
        row_mask = global_rows < step * block_span
        work = apply_update(work, solved, owner, kept_columns[step], row_mask)
    return work


def solution(mesh):
    placed = (P("col", "row"), P("col", "row"), P())
    return jax.shard_map(
        body, mesh=mesh, in_specs=placed, out_specs=P("col", "row"), check_vma=False
    )
```

profile of v0, /device:TPU:0, one launch (start us, length us, event | category | flops | bytes accessed | tf_op | source)
XLA Modules:
  0.0 677.5 jit_solution(9635209791874704113)
XLA Ops:
  7.4 3.0 convolution_select_fusion.7
  10.3 0.0 all-gather.2.cloned.1.call-start
  10.4 0.5 all-gather.2.cloned.1.call-update
  10.9 0.0 all-reduce.11.cloned.1.call-start
  11.0 74.3 %all-reduce.9.cloned.1.call-done = f32[512,128]{1,0:T(8,128)} async-done(((f32[512,128]{1,0:T(8,128)}), f32[512,128]{1,0:T(8,128)}) %all-reduce.9.cloned.1.call-update) | async-done | bytes 262160 | tf_op jit(solution)/shard_map/psum | solution.py:29
  85.3 35.6 %all-gather.2.cloned.1.call-done = bf16[4096,2048]{1,0:T(8,128)(2,1)} async-done(((bf16[4096,512]{1,0:T(8,128)(2,1)}), bf16[4096,2048]{1,0:T(8,128)(2,1)}) %all-gather.2.cloned.1.call-update) | async-done | bytes 16777232 | tf_op jit(solution)/shard_map/all_gather | solution.py:18
  120.9 3.6 fusion.15
  124.6 2.9 convolution_select_fusion.6
  127.5 0.0 all-reduce.11.cloned.1.call-update
  127.5 0.0 all-reduce.13.cloned.1.call-start
  127.6 1.3 slice.106
  129.0 69.8 %all-reduce.11.cloned.1.call-done = f32[512,128]{1,0:T(8,128)} async-done(((f32[512,128]{1,0:T(8,128)}), f32[512,128]{1,0:T(8,128)}) %all-reduce.11.cloned.1.call-update) | async-done | bytes 262160 | tf_op jit(solution)/shard_map/psum | solution.py:29
  198.8 4.1 fusion.13
  202.9 2.9 convolution_select_fusion.5
  205.9 0.0 all-reduce.15.cloned.1.call-start
  205.9 1.3 slice.109
  207.3 68.9 %all-reduce.13.cloned.1.call-done = f32[512,128]{1,0:T(8,128)} async-done(((f32[512,128]{1,0:T(8,128)}), f32[512,128]{1,0:T(8,128)}) %all-reduce.13.cloned.1.call-update) | async-done | bytes 262160 | tf_op jit(solution)/shard_map/psum | solution.py:29
  276.2 4.1 fusion.11
  280.3 2.9 convolution_select_fusion.4
  283.3 0.0 all-reduce.17.cloned.1.call-start
  283.4 1.3 slice.112
  284.7 69.0 %all-reduce.15.cloned.1.call-done = f32[512,128]{1,0:T(8,128)} async-done(((f32[512,128]{1,0:T(8,128)}), f32[512,128]{1,0:T(8,128)}) %all-reduce.15.cloned.1.call-update) | async-done | bytes 262160 | tf_op jit(solution)/shard_map/psum | solution.py:29
  353.7 4.2 fusion.9
  358.0 3.0 convolution_select_fusion.3
  360.9 0.0 all-reduce.17.cloned.1.call-update
  361.0 0.0 all-reduce.19.cloned.1.call-start
  361.0 1.3 slice.115
  362.4 69.0 %all-reduce.17.cloned.1.call-done = f32[512,128]{1,0:T(8,128)} async-done(((f32[512,128]{1,0:T(8,128)}), f32[512,128]{1,0:T(8,128)}) %all-reduce.17.cloned.1.call-update) | async-done | bytes 262160 | tf_op jit(solution)/shard_map/psum | solution.py:29
  431.4 4.2 fusion.7
  435.6 3.0 convolution_select_fusion.2
  438.6 0.2 all-reduce.21.cloned.1.call-start
  438.9 1.3 slice.117
  440.2 68.8 %all-reduce.19.cloned.1.call-done = f32[512,128]{1,0:T(8,128)} async-done(((f32[512,128]{1,0:T(8,128)}), f32[512,128]{1,0:T(8,128)}) %all-reduce.19.cloned.1.call-update) | async-done | bytes 262160 | tf_op jit(solution)/shard_map/psum | solution.py:29
  509.0 4.1 fusion.5
  513.1 3.0 convolution_select_fusion.1
  516.1 0.0 all-reduce.21.cloned.1.call-update
  516.1 0.0 all-reduce.23.cloned.1.call-start
  516.2 1.3 slice.119
  517.5 68.9 %all-reduce.21.cloned.1.call-done = f32[512,128]{1,0:T(8,128)} async-done(((f32[512,128]{1,0:T(8,128)}), f32[512,128]{1,0:T(8,128)}) %all-reduce.21.cloned.1.call-update) | async-done | bytes 262160 | tf_op jit(solution)/shard_map/psum | solution.py:29
  586.5 4.1 fusion.3
  590.6 3.0 convolution_select_fusion
  593.6 0.0 all-reduce.23.cloned.1.call-update
  593.7 1.3 slice.121
  595.0 69.1 %all-reduce.23.cloned.1.call-done = f32[512,128]{1,0:T(8,128)} async-done(((f32[512,128]{1,0:T(8,128)}), f32[512,128]{1,0:T(8,128)}) %all-reduce.23.cloned.1.call-update) | async-done | bytes 262160 | tf_op jit(solution)/shard_map/psum | solution.py:29
  664.1 3.6 fusion.1
  667.6 0.1 slice.123
  667.8 0.8 copy-done.3
  668.6 1.5 pad_maximum_fusion
  (37 shorter events, 0.5 us)
Async XLA Ops:
  7.4 77.9 %all-reduce.9.cloned.1.call-start = ((), (), s32[]{:S(2)}) async-start(), calls=%async_computation | async-start | bytes 524288 | tf_op jit(solution)/shard_map/psum | solution.py:29
  10.3 110.6 %all-gather.2.cloned.1.call-start = ((), (), s32[]{:S(2)}) async-start(), calls=%async_computation.1 | async-start | bytes 20971520 | tf_op jit(solution)/shard_map/all_gather | solution.py:18
  10.9 187.8 %all-reduce.11.cloned.1.call-start = ((), (), s32[]{:S(2)}) async-start(), calls=%async_computation.2 | async-start | bytes 524288 | tf_op jit(solution)/shard_map/psum | solution.py:29
  85.3 39.3 %copy-start = (f32[512,128]{1,0:T(8,128)S(1)}, f32[512,128]{1,0:T(8,128)}, u32[]{:S(2)}) copy-start(f32[512,128]{1,0:T(8,128)} %all-reduce.9.cloned.1.call-done) | copy-start | bytes 786436
  127.5 148.7 %all-reduce.13.cloned.1.call-start = ((), (), s32[]{:S(2)}) async-start(), calls=%async_computation.3 | async-start | bytes 524288 | tf_op jit(solution)/shard_map/psum | solution.py:29
  198.7 4.1 copy-start.2
  205.9 147.8 %all-reduce.15.cloned.1.call-start = ((), (), s32[]{:S(2)}) async-start(), calls=%async_computation.4 | async-start | bytes 524288 | tf_op jit(solution)/shard_map/psum | solution.py:29
  276.2 4.1 copy-start.1
  283.3 148.1 %all-reduce.17.cloned.1.call-start = ((), (), s32[]{:S(2)}) async-start(), calls=%async_computation.5 | async-start | bytes 524288 | tf_op jit(solution)/shard_map/psum | solution.py:29
  353.7 4.2 copy-start.4
  361.0 148.0 %all-reduce.19.cloned.1.call-start = ((), (), s32[]{:S(2)}) async-start(), calls=%async_computation.6 | async-start | bytes 524288 | tf_op jit(solution)/shard_map/psum | solution.py:29
  431.4 4.2 copy-start.5
  438.6 147.8 %all-reduce.21.cloned.1.call-start = ((), (), s32[]{:S(2)}) async-start(), calls=%async_computation.7 | async-start | bytes 524288 | tf_op jit(solution)/shard_map/psum | solution.py:29
  509.0 4.1 copy-start.6
  516.1 147.9 %all-reduce.23.cloned.1.call-start = ((), (), s32[]{:S(2)}) async-start(), calls=%async_computation.8 | async-start | bytes 524288 | tf_op jit(solution)/shard_map/psum | solution.py:29
  586.5 4.1 copy-start.7
  667.6 1.0 copy-start.3
Sparse Core Ops, SparseCore 0:
  11.5 73.7 all-reduce.8
  127.7 71.0 all-reduce.10
  206.0 70.1 all-reduce.12
  283.4 70.2 all-reduce.14
  361.1 70.2 all-reduce.16
  438.8 70.1 all-reduce.18
  516.2 70.1 all-reduce.20
  593.8 70.2 all-reduce.22
Sparse Core Ops, SparseCore 1:
  12.4 108.5 all-gather.1
where the time goes:
time: 678 us
  waiting for transfers between devices  594 us (88%)
  matrix products  55.6 us (8%)
  between operations  15.2 us (2%)
  local copies, waits for them, and re-layouts  10.4 us (2%)
    psum x8, waiting for transfers between devices, solve_block(): solved = lax.psum(jnp.where(owner, product, jnp.float32(0.0)), 'col')  558 us
    all_gather x1, waiting for transfers between devices, body(): panel_rows = lax.all_gather(factors, 'row', axis=1, tiled=True)  35.6 us
    dot_general x8, matrix products, apply_update(): jnp.dot(columns, solved.astype(jnp.bfloat16), preferred_element_type=jnp....  32 us
    dot_general x8, matrix products, solve_block(): jnp.dot(matrix, work[:block], precision=lax.Precision.HIGHEST, preferred_...  23.6 us
  transfers between devices with their start and end apart: 9, of which 9 were waited for; matrix products, arithmetic and copies ran while one was open for 1% of the time, Pallas kernels for 0%

commit v1 on v0

--- a/solution.py
+++ b/solution.py
@@ -26,7 +26,9 @@
             precision=lax.Precision.HIGHEST,
             preferred_element_type=jnp.float32,
         )
-        solved = lax.psum(jnp.where(owner, product, jnp.float32(0.0)), "col")
+        block_2 = jnp.where(owner, product, jnp.float32(0.0))
+        blocks = lax.all_gather(block_2, "col", axis=0, tiled=False)
+        solved = blocks.sum(axis=0)
         return (solved, owner)
 
     def apply_update(work, solved, owner, columns, row_mask):

time: 678 us -> 586 us (0.86)
  waiting for transfers between devices: 594 us -> 489 us
  other arithmetic: 1.82 us -> 15.8 us
    psum x8 -> x0, waiting for transfers between devices: 558 us -> none  [solve_block(): solved = lax.psum(jnp.where(owner, product, jnp.float32(0.0)), 'col')]
    all_gather x0 -> x8, waiting for transfers between devices: none -> 384 us  [solve_block(): blocks = lax.all_gather(block_2, 'col', axis=0, tiled=False)]
    all_gather x1, waiting for transfers between devices: 35.6 us -> 104 us  [body(): panel_rows = lax.all_gather(factors, 'row', axis=1, tiled=True)]
    reduce_sum x0 -> x8, other arithmetic: none -> 14 us  [solve_block(): solved = blocks.sum(axis=0)]
where the time goes in v1:
time: 586 us; the launch traced here: 585 us
  waiting for transfers between devices  489 us (83%)
  matrix products  55.9 us (10%)
  other arithmetic  15.8 us (3%)
  between operations  13.5 us (2%)
  local copies, waits for them, and re-layouts  10.1 us (2%)
    all_gather x8, waiting for transfers between devices, solve_block(): blocks = lax.all_gather(block_2, 'col', axis=0, tiled=False)  384 us
    all_gather x1, waiting for transfers between devices, body(): panel_rows = lax.all_gather(factors, 'row', axis=1, tiled=True)  104 us
    dot_general x8, matrix products, apply_update(): jnp.dot(columns, solved.astype(jnp.bfloat16), preferred_element_type=jnp....  30.8 us
    dot_general x8, matrix products, solve_block(): jnp.dot(matrix, work[:block], precision=lax.Precision.HIGHEST, preferred_...  25.1 us
    reduce_sum x8, other arithmetic, solve_block(): solved = blocks.sum(axis=0)  14 us
  transfers between devices with their start and end apart: 9, of which 9 were waited for; matrix products, arithmetic and copies ran while one was open for 1% of the time, Pallas kernels for 0%

profile of v1, /device:TPU:0, one launch (start us, length us, event | category | flops | bytes accessed | tf_op | source)
XLA Modules:
  0.0 584.6 jit_solution(16530183244064792842)
XLA Ops:
  6.5 3.0 convolution_select_fusion.7
  9.6 0.7 all-gather.18.cloned.1.call-update
  10.3 51.1 %all-gather.20.cloned.1.call-done = f32[4096,128]{1,0:T(8,128)} async-done(((f32[512,128]{1,0:T(8,128)}), f32[4096,128]{1,0:T(8,128)}) %all-gather.20.cloned.1.call-update) | async-done | bytes 2097168 | tf_op jit(solution)/shard_map/all_gather | solution.py:30
  61.5 1.7 reduce_sum.72
  63.2 104.3 %all-gather.18.cloned.1.call-done = bf16[4096,2048]{1,0:T(8,128)(2,1)} async-done(((bf16[4096,512]{1,0:T(8,128)(2,1)}), bf16[4096,2048]{1,0:T(8,128)(2,1)}) %all-gather.18.cloned.1.call-update) | async-done | bytes 16777232 | tf_op jit(solution)/shard_map/all_gather | solution.py:18
  167.5 3.6 fusion.15
  171.1 3.6 convolution_select_fusion.6
  174.8 0.0 all-gather.24.cloned.1.call-start
  174.9 49.2 %all-gather.22.cloned.1.call-done = f32[4096,128]{1,0:T(8,128)} async-done(((f32[512,128]{1,0:T(8,128)}), f32[4096,128]{1,0:T(8,128)}) %all-gather.22.cloned.1.call-update) | async-done | bytes 2097168 | tf_op jit(solution)/shard_map/all_gather | solution.py:30
  224.1 1.8 reduce_sum.73
  225.9 0.3 slice-done
  226.2 4.0 fusion.13
  230.2 1.3 copy-done.1
  231.5 2.9 convolution_select_fusion.5
  234.5 0.0 all-gather.26.cloned.1.call-start
  234.5 47.7 %all-gather.24.cloned.1.call-done = f32[4096,128]{1,0:T(8,128)} async-done(((f32[512,128]{1,0:T(8,128)}), f32[4096,128]{1,0:T(8,128)}) %all-gather.24.cloned.1.call-update) | async-done | bytes 2097168 | tf_op jit(solution)/shard_map/all_gather | solution.py:30
  282.2 1.7 reduce_sum.74
  284.0 4.0 fusion.11
  287.9 1.3 copy-done.2
  289.3 2.9 convolution_select_fusion.4
  292.2 0.0 all-gather.28.cloned.1.call-start
  292.3 47.7 %all-gather.26.cloned.1.call-done = f32[4096,128]{1,0:T(8,128)} async-done(((f32[512,128]{1,0:T(8,128)}), f32[4096,128]{1,0:T(8,128)}) %all-gather.26.cloned.1.call-update) | async-done | bytes 2097168 | tf_op jit(solution)/shard_map/all_gather | solution.py:30
  340.0 1.7 reduce_sum.75
  341.7 4.0 fusion.9
  345.7 1.3 copy-done.6
  347.1 3.0 convolution_select_fusion.3
  350.1 2.9 slice.115
  353.0 44.9 %all-gather.28.cloned.1.call-done = f32[4096,128]{1,0:T(8,128)} async-done(((f32[512,128]{1,0:T(8,128)}), f32[4096,128]{1,0:T(8,128)}) %all-gather.28.cloned.1.call-update) | async-done | bytes 2097168 | tf_op jit(solution)/shard_map/all_gather | solution.py:30
  397.8 1.7 reduce_sum.76
  399.6 3.5 fusion.7
  403.1 3.7 convolution_select_fusion.2
  406.9 0.2 all-gather.32.cloned.1.call-start
  407.1 47.5 %all-gather.30.cloned.1.call-done = f32[4096,128]{1,0:T(8,128)} async-done(((f32[512,128]{1,0:T(8,128)}), f32[4096,128]{1,0:T(8,128)}) %all-gather.30.cloned.1.call-update) | async-done | bytes 2097168 | tf_op jit(solution)/shard_map/all_gather | solution.py:30
  454.6 1.8 reduce_sum.77
  456.5 0.3 slice-done.3
  456.8 3.9 fusion.5
  460.7 1.3 copy-done.4
  462.1 3.0 convolution_select_fusion.1
  465.2 47.7 %all-gather.32.cloned.1.call-done = f32[4096,128]{1,0:T(8,128)} async-done(((f32[512,128]{1,0:T(8,128)}), f32[4096,128]{1,0:T(8,128)}) %all-gather.32.cloned.1.call-update) | async-done | bytes 2097168 | tf_op jit(solution)/shard_map/all_gather | solution.py:30
  512.9 1.7 reduce_sum.78
  514.6 4.0 fusion.3
  518.6 1.3 copy-done.5
  519.9 3.0 convolution_select_fusion
  523.0 47.7 %all-gather.34.cloned.1.call-done = f32[4096,128]{1,0:T(8,128)} async-done(((f32[512,128]{1,0:T(8,128)}), f32[4096,128]{1,0:T(8,128)}) %all-gather.34.cloned.1.call-update) | async-done | bytes 2097168 | tf_op jit(solution)/shard_map/all_gather | solution.py:30
  570.7 1.7 reduce_sum.79
  572.4 4.0 fusion.1
  576.4 0.1 slice.123
  576.6 1.5 pad_maximum_fusion
  (49 shorter events, 0.7 us)
Async XLA Ops:
  6.5 54.9 %all-gather.20.cloned.1.call-start = ((), (), s32[]{:S(2)}) async-start(), calls=%async_computation.1 | async-start | bytes 2359296 | tf_op jit(solution)/shard_map/all_gather | solution.py:30
  9.5 158.0 %all-gather.18.cloned.1.call-start = ((), (), s32[]{:S(2)}) async-start(), calls=%async_computation | async-start | bytes 20971520 | tf_op jit(solution)/shard_map/all_gather | solution.py:18
  10.3 213.8 %all-gather.22.cloned.1.call-start = ((), (), s32[]{:S(2)}) async-start(), calls=%async_computation.2 | async-start | bytes 2359296 | tf_op jit(solution)/shard_map/all_gather | solution.py:30
  171.1 3.8 copy-start
  174.8 107.4 %all-gather.24.cloned.1.call-start = ((), (), s32[]{:S(2)}) async-start(), calls=%async_computation.3 | async-start | bytes 2359296 | tf_op jit(solution)/shard_map/all_gather | solution.py:30
  224.1 2.1 slice-start
  230.1 1.3 copy-start.1
  234.5 105.5 %all-gather.26.cloned.1.call-start = ((), (), s32[]{:S(2)}) async-start(), calls=%async_computation.4 | async-start | bytes 2359296 | tf_op jit(solution)/shard_map/all_gather | solution.py:30
  234.5 49.4 %slice-start.1 = ((f32[4096,128]{1,0:T(8,128)}), f32[3584,128]{1,0:T(8,128)S(1)}, s32[]{:S(2)}) async-start(f32[4096,128]{1,0:T(8,128)} %copy-done.1), calls=%async_computation.10 | async-start | bytes 3670016 | tf_op jit(solution)/shard_map/slice | solution.py:38
  287.9 1.3 copy-start.2
  292.2 105.6 %all-gather.28.cloned.1.call-start = ((), (), s32[]{:S(2)}) async-start(), calls=%async_computation.5 | async-start | bytes 2359296 | tf_op jit(solution)/shard_map/all_gather | solution.py:30
  292.3 49.4 %slice-start.2 = ((f32[4096,128]{1,0:T(8,128)}), f32[3584,128]{1,0:T(8,128)S(1)}, s32[]{:S(2)}) async-start(f32[4096,128]{1,0:T(8,128)} %copy-done.2), calls=%async_computation.11 | async-start | bytes 3670016 | tf_op jit(solution)/shard_map/slice | solution.py:38
  345.7 1.3 copy-start.6
  350.1 104.6 %all-gather.30.cloned.1.call-start = ((), (), s32[]{:S(2)}) async-start(), calls=%async_computation.6 | async-start | bytes 2359296 | tf_op jit(solution)/shard_map/all_gather | solution.py:30
  403.1 4.0 copy-start.3
  406.9 106.0 %all-gather.32.cloned.1.call-start = ((), (), s32[]{:S(2)}) async-start(), calls=%async_computation.7 | async-start | bytes 2359296 | tf_op jit(solution)/shard_map/all_gather | solution.py:30
  454.6 2.1 slice-start.3
  460.7 1.3 copy-start.4
  465.1 105.6 %all-gather.34.cloned.1.call-start = ((), (), s32[]{:S(2)}) async-start(), calls=%async_computation.8 | async-start | bytes 2359296 | tf_op jit(solution)/shard_map/all_gather | solution.py:30
  465.2 49.4 %slice-start.4 = ((f32[4096,128]{1,0:T(8,128)}), f32[3584,128]{1,0:T(8,128)S(1)}, s32[]{:S(2)}) async-start(f32[4096,128]{1,0:T(8,128)} %copy-done.4), calls=%async_computation.13 | async-start | bytes 3670016 | tf_op jit(solution)/shard_map/slice | solution.py:38
  518.6 1.3 copy-start.5
  522.9 49.5 %slice-start.5 = ((f32[4096,128]{1,0:T(8,128)}), f32[3584,128]{1,0:T(8,128)S(1)}, s32[]{:S(2)}) async-start(f32[4096,128]{1,0:T(8,128)} %copy-done.5), calls=%async_computation.14 | async-start | bytes 3670016 | tf_op jit(solution)/shard_map/slice | solution.py:38
Sparse Core Ops, SparseCore 0:
  9.6 51.7 all-gather.19
  63.0 104.4 all-gather.17
  174.9 49.0 all-gather.21
  234.6 47.6 all-gather.23
  292.4 47.5 all-gather.25
  350.2 47.6 all-gather.27
  407.0 47.6 all-gather.29
  465.2 47.6 all-gather.31
  523.1 47.6 all-gather.33
